TPU v7x, 32 devices: a whole 2x2x4 slice. The times are simulated.
32 devices in a mesh: seq: 16 (over z, y, core), dp: 2 (over x).
Axes of the slice: x: 2, y: 2, z: 4, core: 2. Of those that a mesh axis runs over, the one named last changes fastest.
Arguments:
- queries: bfloat16 [2, 4096, 2048], P('dp', 'seq'), may hold values from -6 to 6
- key_rows: bfloat16 [2, 4096, 2048], P('dp', 'seq'), may hold values from -6 to 6
- value_rows: bfloat16 [2, 4096, 2048], P('dp', 'seq'), may hold values from -6 to 6
- out_grad: bfloat16 [2, 4096, 2048], P('dp', 'seq'), may hold values from -6 to 6
- out_weight: bfloat16 [2048, 2048], P('seq', 'dp'), may hold values from -0.125 to 0.125
Outputs:
- query_grad: bfloat16 [2, 4096, 2048], P('dp', 'seq')
- key_grad: bfloat16 [2, 4096, 2048], P('dp', 'seq')
- value_grad: bfloat16 [2, 4096, 2048], P('dp', 'seq')
- weight_grad: float32 [2048, 2048], P('seq', 'dp')
All inputs are finite; a program needn't handle non-finite values.
Results may differ from a plain program's by a relative error of at most 0.014.
Values may be sent and summed in bfloat16 or wider, within the bound.
A program may use at most 192 MiB of HBM per device.

v0:
```python
import math
import jax
import jax.numpy as jnp
from jax import lax
from jax.sharding import PartitionSpec as P

HEADS = 16
HEAD = 128
HD = 2048


def exchanged_sums(part, scale, axis, reverse):
    count = lax.axis_size(axis)
    heads, depth, width = part.shape
    rows = part.reshape(heads * depth, width).astype(jnp.bfloat16)
    mine = lax.all_to_all(rows, axis, 0, 0, tiled=True)
    mine = mine.reshape(count, -1, width).astype(jnp.float32)
    order = range(count - 1, -1, -1) if reverse else range(count)
    state = jnp.zeros_like(mine[0])
    sums = [None] * count
    for source in order:
        sums[source] = (scale * state).astype(jnp.bfloat16)
        state = state + mine[source]
    back = lax.all_to_all(jnp.concatenate(sums, axis=0), axis, 0, 0, tiled=True)
    return back.reshape(heads, depth, width)


def shards(queries, key_rows, value_rows, out_grad, out_weight):
    tokens_dev = queries.shape[1]
    seq_devices = lax.axis_size("seq")
    data_devices = lax.axis_size("dp")
    seq_length = tokens_dev * seq_devices
    seq_count = queries.shape[0] * data_devices
    score_scale = 1.0 / math.sqrt(HEAD * seq_length)
    grad_scale = 1.0 / math.sqrt(seq_count * seq_length)
    query_flat = queries[0]
    grad_flat = out_grad[0]
    query_h = query_flat.reshape(tokens_dev, HEADS, HEAD)
    key_h = key_rows[0].reshape(tokens_dev, HEADS, HEAD)
    value_h = value_rows[0].reshape(tokens_dev, HEADS, HEAD)
    row_ids = lax.broadcasted_iota(jnp.int32, (tokens_dev, tokens_dev), 0)
    col_ids = lax.broadcasted_iota(jnp.int32, (tokens_dev, tokens_dev), 1)
    causal = (row_ids >= col_ids).astype(jnp.float32)
    kv_local = jnp.einsum("shd,she->hde", key_h, value_h, preferred_element_type=jnp.float32)
    wide_weight = lax.all_gather(out_weight, "dp", axis=1, tiled=True)
    head_grad = lax.dot_general(
        grad_flat,
        lax.all_gather(wide_weight, "seq", axis=0, tiled=True),
        (((1,), (1,)), ((), ())),
        preferred_element_type=jnp.float32,
    ).astype(jnp.bfloat16)
    grad_h = head_grad.reshape(tokens_dev, HEADS, HEAD)
    query_dout = jnp.einsum("thd,the->hde", query_h, grad_h, preferred_element_type=jnp.float32)
    prefix_scaled = exchanged_sums(kv_local, score_scale, "seq", False)
    suffix_scaled = exchanged_sums(query_dout, score_scale, "seq", True)
    scores = (
        score_scale
        * jnp.einsum("thd,shd->hts", query_h, key_h, preferred_element_type=jnp.float32)
        * causal
    ).astype(jnp.bfloat16)
    attended = jnp.einsum("hts,shd->thd", scores, value_h, preferred_element_type=jnp.float32)
    attended = attended + jnp.einsum(
        "thd,hde->the", query_h, prefix_scaled, preferred_element_type=jnp.float32
    )
    attended = attended.astype(jnp.bfloat16).reshape(tokens_dev, HD)
    row_sums = lax.psum_scatter(
        (
            grad_scale
            * lax.dot_general(
                attended, grad_flat, (((0,), (0,)), ((), ())), preferred_element_type=jnp.float32
            )
        ).astype(jnp.bfloat16),
        "seq",
        scatter_dimension=0,
        tiled=True,
    )
    weight_grad = lax.psum_scatter(row_sums, "dp", scatter_dimension=1, tiled=True).astype(
        jnp.float32
    )
    grad_scores = (
        score_scale
        * jnp.einsum("the,she->hts", grad_h, value_h, preferred_element_type=jnp.float32)
        * causal
    ).astype(jnp.bfloat16)
    query_g = jnp.einsum("hts,shd->thd", grad_scores, key_h, preferred_element_type=jnp.float32)
    query_g = query_g + jnp.einsum(
        "the,hde->thd", grad_h, prefix_scaled, preferred_element_type=jnp.float32
    )
    key_g = jnp.einsum("hts,thd->shd", grad_scores, query_h, preferred_element_type=jnp.float32)
    key_g = key_g + jnp.einsum(
        "she,hde->shd", value_h, suffix_scaled, preferred_element_type=jnp.float32
    )
    value_g = jnp.einsum("hts,the->she", scores, grad_h, preferred_element_type=jnp.float32)
    value_g = value_g + jnp.einsum(
        "shd,hde->she", key_h, suffix_scaled, preferred_element_type=jnp.float32
    )
    query_grad = query_g.astype(jnp.bfloat16).reshape(1, tokens_dev, HD)
    key_grad = key_g.astype(jnp.bfloat16).reshape(1, tokens_dev, HD)
    value_grad = value_g.astype(jnp.bfloat16).reshape(1, tokens_dev, HD)
    return (query_grad, key_grad, value_grad, weight_grad)


def solution(mesh):
    return jax.shard_map(
        shards,
        mesh=mesh,
        in_specs=(
            P("dp", "seq", None),
            P("dp", "seq", None),
            P("dp", "seq", None),
            P("dp", "seq", None),
            P("seq", "dp"),
        ),
        out_specs=(
            P("dp", "seq", None),
            P("dp", "seq", None),
            P("dp", "seq", None),
            P("seq", "dp"),
        ),
        check_vma=False,
    )
```

profile of v0, /device:TPU:0, one launch (start us, length us, event | category | flops | bytes accessed | tf_op | source)
XLA Modules:
  0.0 319.2 jit_solution(4573787005507438147)
XLA Ops:
  7.2 1.5 copy.36
  8.7 1.5 copy.35
  10.2 1.3 convolution_convert_fusion.2
  11.5 7.4 %all-to-all-start = ((bf16[16,128,128]{2,1,0:T(8,128)(2,1)}), bf16[16,128,128]{2,1,0:T(8,128)(2,1)}, u32[]{:S(2)}, u32[]{:S(2)}) async-start(bf16[16,128,128]{2,1,0:T(8,128)(2,1)} %convolution_convert_fusion.2), calls=%async_computation | async-start | bytes 1048576 | tf_op jit(solution)/shard_map/all_to_all | solution.py:16
  19.6 13.9 %all-to-all-done = bf16[16,128,128]{2,1,0:T(8,128)(2,1)} async-done(((bf16[16,128,128]{2,1,0:T(8,128)(2,1)}), bf16[16,128,128]{2,1,0:T(8,128)(2,1)}, u32[]{:S(2)}, u32[]{:S(2)}) %all-to-all-start) | async-done | bytes 524320 | tf_op jit(solution)/shard_map/all_to_all | solution.py:16
  33.5 1.1 convert_element_type.159
  34.6 0.6 constant_dynamic-update-slice_fusion.14
  35.2 0.6 constant_dynamic-update-slice_fusion.13
  35.9 0.6 constant_dynamic-update-slice_fusion.12
  36.5 0.6 constant_dynamic-update-slice_fusion.11
  37.7 0.6 constant_dynamic-update-slice_fusion.9
  39.0 0.6 constant_dynamic-update-slice_fusion.7
  40.3 0.6 constant_dynamic-update-slice_fusion.5
  41.5 0.6 constant_dynamic-update-slice_fusion.3
  42.8 0.6 constant_dynamic-update-slice_fusion.1
  43.4 0.6 constant_dynamic-update-slice_fusion
  44.0 4.2 %all-to-all-start.1 = ((bf16[16,128,128]{2,1,0:T(8,128)(2,1)}), bf16[16,128,128]{2,1,0:T(8,128)(2,1)}, u32[]{:S(2)}, u32[]{:S(2)}) async-start(bf16[16,128,128]{2,1,0:T(8,128)(2,1)} %bitcast.201), calls=%async_computation.1 | async-start | bytes 1048576 | tf_op jit(solution)/shard_map/all_to_all | solution.py:24
  48.3 1.5 copy.37
  49.8 0.7 multiply_convert_fusion.1
  50.8 1.3 copy-done.3
  52.1 2.2 fusion.52
  54.3 8.4 %all-to-all-done.1 = bf16[16,128,128]{2,1,0:T(8,128)(2,1)} async-done(((bf16[16,128,128]{2,1,0:T(8,128)(2,1)}), bf16[16,128,128]{2,1,0:T(8,128)(2,1)}, u32[]{:S(2)}, u32[]{:S(2)}) %all-to-all-start.1) | async-done | bytes 524320 | tf_op jit(solution)/shard_map/all_to_all | solution.py:24
  62.7 2.6 fusion
  65.3 5.6 %multiply_convert_fusion = bf16[2048,2048]{1,0:T(8,128)(2,1)} fusion(bf16[256,2048]{0,1:T(8,128)(2,1)S(1)} %bitcast.200, bf16[1,256,2048]{2,1,0:T(8,128)(2,1)S(1)} %copy-done), kind=kOutput, calls=%fused_computation | convolution fusion | flops 2155872256 | bytes 10485760 | tf_op jit(solution)/shard_map/dot_general | solution.py:69
  71.0 10.6 %all_gather.6 = bf16[128,2048]{1,0:T(8,128)(2,1)} all-gather(bf16[128,1024]{1,0:T(8,128)(2,1)} %param.9), channel_id=1, replica_groups=mesh['seq'=16,'dp'=2] {'dp'}, dimensions={1}, use_global_device_ids=true | all-gather | bytes 786432 | tf_op jit(solution)/shard_map/all_gather | solution.py:45
  81.7 93.4 %reduce-scatter.3.cloned.1.call-done = bf16[128,2048]{1,0:T(8,128)(2,1)} async-done(((bf16[2048,2048]{1,0:T(8,128)(2,1)}), bf16[128,2048]{1,0:T(8,128)(2,1)}) %reduce-scatter.3.cloned.1.call-update) | async-done | bytes 524304 | tf_op jit(solution)/shard_map/reduce_scatter | solution.py:66
  175.1 76.8 %all-gather.2.cloned.1.call-done = bf16[2048,2048]{1,0:T(8,128)(2,1)} async-done(((bf16[128,2048]{1,0:T(8,128)(2,1)}), bf16[2048,2048]{1,0:T(8,128)(2,1)}) %all-gather.2.cloned.1.call-update) | async-done | bytes 8388624 | tf_op jit(solution)/shard_map/all_gather | solution.py:48
  251.9 6.7 %convolution_convert_fusion = bf16[256,2048]{1,0:T(8,128)(2,1)} fusion(bf16[2048,2048]{1,0:T(8,128)(2,1)} %all-gather.2.cloned.1.call-done, bf16[1,256,2048]{2,1,0:T(8,128)(2,1)S(1)} %copy-done), kind=kOutput, calls=%fused_computation.3 | convolution fusion | flops 2148007936 | bytes 10485760 | tf_op jit(solution)/shard_map/dot_general | solution.py:46
  258.6 2.3 copy.34
  260.9 2.8 fusion.3
  263.7 4.3 %all-to-all-start.2 = ((bf16[16,128,128]{2,1,0:T(8,128)(2,1)}), bf16[16,128,128]{2,1,0:T(8,128)(2,1)}, u32[]{:S(2)}, u32[]{:S(2)}) async-start(bf16[16,128,128]{2,1,0:T(8,128)(2,1)} %fusion.3), calls=%async_computation.2 | async-start | bytes 1048576 | tf_op jit(solution)/shard_map/all_to_all | solution.py:16
  268.0 1.8 convert_element_type.204
  269.8 2.0 multiply_convert_fusion.2
  271.8 1.3 copy-done.4
  273.1 2.1 fusion.7
  275.2 7.2 %all-to-all-done.2 = bf16[16,128,128]{2,1,0:T(8,128)(2,1)} async-done(((bf16[16,128,128]{2,1,0:T(8,128)(2,1)}), bf16[16,128,128]{2,1,0:T(8,128)(2,1)}, u32[]{:S(2)}, u32[]{:S(2)}) %all-to-all-start.2) | async-done | bytes 524320 | tf_op jit(solution)/shard_map/all_to_all | solution.py:16
  282.4 1.1 convert_element_type.180
  284.0 0.8 copy-done.6
  284.8 4.4 %all-to-all-start.3 = ((bf16[16,128,128]{2,1,0:T(8,128)(2,1)}), bf16[16,128,128]{2,1,0:T(8,128)(2,1)}, u32[]{:S(2)}, u32[]{:S(2)}) async-start(bf16[16,128,128]{2,1,0:T(8,128)(2,1)} %bitcast.202), calls=%async_computation.3 | async-start | bytes 1048576 | tf_op jit(solution)/shard_map/all_to_all | solution.py:24
  289.3 3.5 %fusion.2 = bf16[256,16,128]{0,2,1:T(8,128)(2,1)} fusion(f32[16,256,128]{1,2,0:T(8,128)} %fusion.7, bf16[16,128,128]{2,1,0:T(8,128)(2,1)} %all-to-all-done.1, bf16[256,16,128]{0,2,1:T(8,128)(2,1)} %bitcast.193), kind=kOutput, calls=%fused_computation.9 | convolution fusion | flops 135266304 | bytes 4718592 | tf_op jit(solution)/shard_map/the,hde->thd/dot_general | solution.py:86
  292.7 2.3 copy.28
  295.0 3.8 %fusion.51 = f32[16,128,256]{2,1,0:T(8,128)} fusion(bf16[256,16,128]{0,2,1:T(8,128)(2,1)} %bitcast.194, bf16[16,256,256]{2,1,0:T(8,128)(2,1)} %copy-done.3), kind=kOutput, calls=%fused_computation.150 | convolution fusion | flops 268435456 | bytes 5242880 | tf_op jit(solution)/shard_map/hts,the->she/dot_general | solution.py:93
  298.8 1.9 fusion.11
  300.7 2.8 all-to-all-done.3
  303.5 3.2 %add_convert_fusion = bf16[16,128,256]{2,1,0:T(8,128)(2,1)} fusion(f32[16,128,256]{2,1,0:T(8,128)} %fusion.51, bf16[16,128,128]{2,1,0:T(8,128)(2,1)} %all-to-all-done.3, bf16[256,16,128]{2,1,0:T(8,128)(2,1)S(1)} %bitcast.186), kind=kOutput, calls=%fused_computation.10 | convolution fusion | flops 135266304 | bytes 4718592 | tf_op jit(solution)/shard_map/shd,hde->she/dot_general | solution.py:94
  306.8 2.3 copy.30
  309.1 2.2 fusion.1
  311.3 1.4 copy.29
  (41 shorter events, 4.6 us)
Async XLA Ops:
  7.2 58.2 %copy-start = (bf16[1,256,2048]{2,1,0:T(8,128)(2,1)S(1)}, bf16[1,256,2048]{2,1,0:T(8,128)(2,1)}, u32[]{:S(2)}) copy-start(bf16[1,256,2048]{2,1,0:T(8,128)(2,1)} %param.8) | copy-start | bytes 3145732
  11.5 22.0 %all-to-all-start = ((bf16[16,128,128]{2,1,0:T(8,128)(2,1)}), bf16[16,128,128]{2,1,0:T(8,128)(2,1)}, u32[]{:S(2)}, u32[]{:S(2)}) async-start(bf16[16,128,128]{2,1,0:T(8,128)(2,1)} %convolution_convert_fusion.2), calls=%async_computation | async-start | bytes 1048576 | tf_op jit(solution)/shard_map/all_to_all | solution.py:16
  44.0 18.7 %all-to-all-start.1 = ((bf16[16,128,128]{2,1,0:T(8,128)(2,1)}), bf16[16,128,128]{2,1,0:T(8,128)(2,1)}, u32[]{:S(2)}, u32[]{:S(2)}) async-start(bf16[16,128,128]{2,1,0:T(8,128)(2,1)} %bitcast.201), calls=%async_computation.1 | async-start | bytes 1048576 | tf_op jit(solution)/shard_map/all_to_all | solution.py:24
  48.3 126.8 %reduce-scatter.3.cloned.1.call-start = ((), (), s32[]{:S(2)}) async-start(), calls=%async_computation.7 | async-start | bytes 8912896 | tf_op jit(solution)/shard_map/reduce_scatter | solution.py:66
  49.8 1.0 copy-start.1
  50.8 1.3 copy-start.3
  70.9 181.0 %all-gather.2.cloned.1.call-start = ((), (), s32[]{:S(2)}) async-start(), calls=%async_computation.6 | async-start | bytes 8912896 | tf_op jit(solution)/shard_map/all_gather | solution.py:48
  81.7 186.3 %reduce-scatter.5.cloned.1.call-start = ((), (), s32[]{:S(2)}) async-start(), calls=%async_computation.8 | async-start | bytes 786432 | tf_op jit(solution)/shard_map/reduce_scatter | solution.py:77
  263.7 18.7 %all-to-all-start.2 = ((bf16[16,128,128]{2,1,0:T(8,128)(2,1)}), bf16[16,128,128]{2,1,0:T(8,128)(2,1)}, u32[]{:S(2)}, u32[]{:S(2)}) async-start(bf16[16,128,128]{2,1,0:T(8,128)(2,1)} %fusion.3), calls=%async_computation.2 | async-start | bytes 1048576 | tf_op jit(solution)/shard_map/all_to_all | solution.py:16
  271.8 1.3 copy-start.4
  284.0 0.8 copy-start.6
  284.8 18.7 %all-to-all-start.3 = ((bf16[16,128,128]{2,1,0:T(8,128)(2,1)}), bf16[16,128,128]{2,1,0:T(8,128)(2,1)}, u32[]{:S(2)}, u32[]{:S(2)}) async-start(bf16[16,128,128]{2,1,0:T(8,128)(2,1)} %bitcast.202), calls=%async_computation.3 | async-start | bytes 1048576 | tf_op jit(solution)/shard_map/all_to_all | solution.py:24
  295.0 3.8 %copy-start.2 = (bf16[32,8,16,128]{3,2,1,0:T(8,128)(2,1)S(1)}, bf16[32,8,16,128]{3,2,1,0:T(8,128)(2,1)}, u32[]{:S(2)}) copy-start(bf16[32,8,16,128]{3,2,1,0:T(8,128)(2,1)} %copy-done.1) | copy-start | bytes 3145732
  295.0 3.8 %copy-start.5 = (bf16[16,256,256]{2,1,0:T(8,128)(2,1)S(1)}, bf16[16,256,256]{2,1,0:T(8,128)(2,1)}, u32[]{:S(2)}) copy-start(bf16[16,256,256]{2,1,0:T(8,128)(2,1)} %copy-done.4) | copy-start | bytes 6291460
Sparse Core Ops, SparseCore 0:
  71.1 103.9 reduce-scatter.2
  177.2 74.6 all-gather.1
  254.2 12.7 reduce-scatter.4
where the time goes:
time: 320 us; the launch traced here: 319 us
  waiting for transfers between devices  203 us (63%)
  matrix products  40.6 us (13%)
  starting transfers between devices  20.5 us (6%)
  local copies, waits for them, and re-layouts  17 us (5%)
  between operations  14 us (4%)
  other arithmetic  13.8 us (4%)
  blocking collectives  10.6 us (3%)
    reduce_scatter x1, waiting for transfers between devices, shards(): lax.psum_scatter((grad_scale * lax.dot_general(attended, grad_flat, (((0,...  93.4 us
    all_gather x1, waiting for transfers between devices, shards(): lax.all_gather(wide_weight, 'seq', axis=0, tiled=True)  76.8 us
    all_to_all x2, waiting for transfers between devices, exchanged_sums(): mine = lax.all_to_all(rows, axis, 0, 0, tiled=True)  21.1 us
    unnamed x20, local copies, waits for them, and re-layouts  13.3 us
    all_to_all x2, starting transfers between devices, exchanged_sums(): mine = lax.all_to_all(rows, axis, 0, 0, tiled=True)  11.7 us
    all_to_all x2, waiting for transfers between devices, exchanged_sums(): back = lax.all_to_all(jnp.concatenate(sums, axis=0), axis, 0, 0, tiled=True)  11.3 us
    all_gather x1, blocking collectives, shards(): wide_weight = lax.all_gather(out_weight, 'dp', axis=1, tiled=True)  10.6 us
    unnamed x29, other arithmetic  9.13 us
  transfers between devices with their start and end apart: 7, of which 6 were waited for; matrix products, arithmetic and copies ran while one was open for 11% of the time, Pallas kernels for 0%

commit v1 on v0

--- a/solution.py
+++ b/solution.py
@@ -7,6 +7,19 @@
 HEADS = 16
 HEAD = 128
 HD = 2048
+
+
+def gather_around(array, axis, dim):
+    ways = lax.axis_size(axis)
+    up = [(d, (d + 1) % ways) for d in range(ways)]
+    down = [(d, (d - 1) % ways) for d in range(ways)]
+    earlier, later = ([array], [array])
+    for _ in range(ways // 2):
+        earlier.append(lax.ppermute(earlier[-1], axis, up))
+    for _ in range((ways - 1) // 2):
+        later.append(lax.ppermute(later[-1], axis, down))
+    line = jnp.concatenate([*earlier[::-1], *later[1:]], axis=dim)
+    return jnp.roll(line, (lax.axis_index(axis) - ways // 2) * array.shape[dim], axis=dim)
 
 
 def exchanged_sums(part, scale, axis, reverse):
@@ -45,7 +58,7 @@
     wide_weight = lax.all_gather(out_weight, "dp", axis=1, tiled=True)
     head_grad = lax.dot_general(
         grad_flat,
-        lax.all_gather(wide_weight, "seq", axis=0, tiled=True),
+        gather_around(wide_weight, "seq", 0),
         (((1,), (1,)), ((), ())),
         preferred_element_type=jnp.float32,
     ).astype(jnp.bfloat16)

time: 320 us -> 284 us (0.89)
  waiting for transfers between devices: 203 us -> 81.3 us
  starting transfers between devices: 20.5 us -> 75.6 us
  local copies, waits for them, and re-layouts: 17 us -> 43.8 us
    all_gather x1 -> x0, waiting for transfers between devices: 76.8 us -> none  [shards(): lax.all_gather(wide_weight, 'seq', axis=0, tiled=True)]
    reduce_scatter x1, waiting for transfers between devices: 93.4 us -> 36.6 us  [shards(): lax.psum_scatter((grad_scale * lax.dot_general(attended, grad_flat, (((0,...]
    ppermute x0 -> x15, starting transfers between devices: none -> 43.2 us  [the longest x7 21.7 us: gather_around(): later.append(lax.ppermute(later[-1], axis, down))]
    unnamed x20 -> x59, local copies, waits for them, and re-layouts: 13.3 us -> 42.3 us
    ppermute x0 -> x15, waiting for transfers between devices: none -> 28.6 us  [the longest x8 25.2 us: gather_around(): earlier.append(lax.ppermute(earlier[-1], axis, up))]
    all_to_all x2, waiting for transfers between devices: 11.3 us -> 0.01 us  [exchanged_sums(): back = lax.all_to_all(jnp.concatenate(sums, axis=0), axis, 0, 0, tiled=True)]
    all_to_all x2, starting transfers between devices: 8.67 us -> 18.3 us  [exchanged_sums(): back = lax.all_to_all(jnp.concatenate(sums, axis=0), axis, 0, 0, tiled=True)]
    all_to_all x2, waiting for transfers between devices: 21.1 us -> 16.1 us  [exchanged_sums(): mine = lax.all_to_all(rows, axis, 0, 0, tiled=True)]
  transfers between devices with their start and end apart: 7 -> 21, of which waited for: 6 -> 9; matrix products, arithmetic and copies ran while one was open for 11% -> 33% of each run, Pallas kernels for 0% -> 0%
where the time goes in v1:
time: 284 us; the launch traced here: 281 us
  waiting for transfers between devices  81.3 us (29%)
  starting transfers between devices  75.6 us (27%)
  local copies, waits for them, and re-layouts  43.8 us (15%)
  matrix products  42.8 us (15%)
  between operations  14.5 us (5%)
  other arithmetic  13.9 us (5%)
  blocking collectives  9.45 us (3%)
    unnamed x59, local copies, waits for them, and re-layouts  42.3 us
    reduce_scatter x1, waiting for transfers between devices, shards(): lax.psum_scatter((grad_scale * lax.dot_general(attended, grad_flat, (((0,...  36.6 us
    ppermute x8, waiting for transfers between devices, gather_around(): earlier.append(lax.ppermute(earlier[-1], axis, up))  25.2 us
    ppermute x7, starting transfers between devices, gather_around(): later.append(lax.ppermute(later[-1], axis, down))  21.7 us
    ppermute x8, starting transfers between devices, gather_around(): earlier.append(lax.ppermute(earlier[-1], axis, up))  21.5 us
    all_to_all x2, starting transfers between devices, exchanged_sums(): back = lax.all_to_all(jnp.concatenate(sums, axis=0), axis, 0, 0, tiled=True)  18.3 us
    all_to_all x2, waiting for transfers between devices, exchanged_sums(): mine = lax.all_to_all(rows, axis, 0, 0, tiled=True)  16.1 us
    all_to_all x2, starting transfers between devices, exchanged_sums(): mine = lax.all_to_all(rows, axis, 0, 0, tiled=True)  14 us
  transfers between devices with their start and end apart: 21, of which 9 were waited for; matrix products, arithmetic and copies ran while one was open for 33% of the time, Pallas kernels for 0%

profile of v1, /device:TPU:0, one launch (start us, length us, event | category | flops | bytes accessed | tf_op | source)
XLA Modules:
  0.0 281.3 jit_solution(15027212511141080659)
XLA Ops:
  7.2 1.5 copy.35
  8.7 1.5 copy.34
  10.2 1.3 convolution_convert_fusion.1
  11.5 7.4 %all-to-all-start = ((bf16[16,128,128]{2,1,0:T(8,128)(2,1)}), bf16[16,128,128]{2,1,0:T(8,128)(2,1)}, u32[]{:S(2)}, u32[]{:S(2)}) async-start(bf16[16,128,128]{2,1,0:T(8,128)(2,1)} %convolution_convert_fusion.1), calls=%async_computation | async-start | bytes 1048576 | tf_op jit(solution)/shard_map/all_to_all | solution.py:29
  18.9 9.4 %all_gather.3 = bf16[128,2048]{1,0:T(8,128)(2,1)S(1)} all-gather(bf16[128,1024]{1,0:T(8,128)(2,1)} %param.9), channel_id=1, replica_groups=mesh['seq'=16,'dp'=2] {'dp'}, dimensions={1}, use_global_device_ids=true | all-gather | bytes 786432 | tf_op jit(solution)/shard_map/all_gather | solution.py:58
  29.2 3.7 %collective-permute-start.8 = (bf16[128,2048]{1,0:T(8,128)(2,1)S(1)}, bf16[128,2048]{1,0:T(8,128)(2,1)}, u32[]{:S(2)}, u32[]{:S(2)}) collective-permute-start(bf16[128,2048]{1,0:T(8,128)(2,1)S(1)} %all_gather.3), channel_id=1, source_target_pairs={{0,30},{2,0},{4,2},{6,4},{8,6},{10,8},{12,10},{14,12},{16,14},{18,... | collective-permute-start | bytes 1572872 | tf_op jit(solution)/shard_map/ppermute | solution.py:20
  33.5 6.5 %collective-permute-done = bf16[128,2048]{1,0:T(8,128)(2,1)} collective-permute-done((bf16[128,2048]{1,0:T(8,128)(2,1)S(1)}, bf16[128,2048]{1,0:T(8,128)(2,1)}, u32[]{:S(2)}, u32[]{:S(2)}) %collective-permute-start) | collective-permute-done | bytes 524320 | tf_op jit(solution)/shard_map/ppermute | solution.py:18
  40.0 2.7 collective-permute-start.1
  42.6 1.8 collective-permute-start.9
  48.1 3.6 %collective-permute-done.1 = bf16[128,2048]{1,0:T(8,128)(2,1)} collective-permute-done((bf16[128,2048]{1,0:T(8,128)(2,1)}, bf16[128,2048]{1,0:T(8,128)(2,1)}, u32[]{:S(2)}, u32[]{:S(2)}) %collective-permute-start.1) | collective-permute-done | bytes 524320 | tf_op jit(solution)/shard_map/ppermute | solution.py:18
  51.7 4.6 %collective-permute-start.2 = (bf16[128,2048]{1,0:T(8,128)(2,1)}, bf16[128,2048]{1,0:T(8,128)(2,1)S(1)}, u32[]{:S(2)}, u32[]{:S(2)}) collective-permute-start(bf16[128,2048]{1,0:T(8,128)(2,1)} %collective-permute-done.1), channel_id=1, source_target_pairs={{0,2},{2,4},{4,6},{6,8},{8,10},{10,12},{12,14},{14,16},{16,18},{18... | collective-permute-start | bytes 1572872 | tf_op jit(solution)/shard_map/ppermute | solution.py:18
  58.2 5.0 %collective-permute-done.2 = bf16[128,2048]{1,0:T(8,128)(2,1)S(1)} collective-permute-done((bf16[128,2048]{1,0:T(8,128)(2,1)}, bf16[128,2048]{1,0:T(8,128)(2,1)S(1)}, u32[]{:S(2)}, u32[]{:S(2)}) %collective-permute-start.2) | collective-permute-done | bytes 524320 | tf_op jit(solution)/shard_map/ppermute | solution.py:18
  63.2 2.0 collective-permute-start.3
  67.1 2.4 collective-permute-start.10
  69.5 5.1 %collective-permute-done.3 = bf16[128,2048]{1,0:T(8,128)(2,1)S(1)} collective-permute-done((bf16[128,2048]{1,0:T(8,128)(2,1)S(1)}, bf16[128,2048]{1,0:T(8,128)(2,1)S(1)}, u32[]{:S(2)}, u32[]{:S(2)}) %collective-permute-start.3) | collective-permute-done | bytes 524320 | tf_op jit(solution)/shard_map/ppermute | solution.py:18
  74.6 4.7 %collective-permute-start.4 = (bf16[128,2048]{1,0:T(8,128)(2,1)S(1)}, bf16[128,2048]{1,0:T(8,128)(2,1)}, u32[]{:S(2)}, u32[]{:S(2)}) collective-permute-start(bf16[128,2048]{1,0:T(8,128)(2,1)S(1)} %collective-permute-done.3), channel_id=1, source_target_pairs={{0,2},{2,4},{4,6},{6,8},{8,10},{10,12},{12,14},{14,16},{16,18},{18... | collective-permute-start | bytes 1572872 | tf_op jit(solution)/shard_map/ppermute | solution.py:18
  81.3 4.8 %collective-permute-done.4 = bf16[128,2048]{1,0:T(8,128)(2,1)} collective-permute-done((bf16[128,2048]{1,0:T(8,128)(2,1)S(1)}, bf16[128,2048]{1,0:T(8,128)(2,1)}, u32[]{:S(2)}, u32[]{:S(2)}) %collective-permute-start.4) | collective-permute-done | bytes 524320 | tf_op jit(solution)/shard_map/ppermute | solution.py:18
  86.0 7.5 %collective-permute-start.5 = (bf16[128,2048]{1,0:T(8,128)(2,1)}, bf16[128,2048]{1,0:T(8,128)(2,1)}, u32[]{:S(2)}, u32[]{:S(2)}) collective-permute-start(bf16[128,2048]{1,0:T(8,128)(2,1)} %collective-permute-done.4), channel_id=1, source_target_pairs={{0,2},{2,4},{4,6},{6,8},{8,10},{10,12},{12,14},{14,16},{16,18},{18... | collective-permute-start | bytes 1572872 | tf_op jit(solution)/shard_map/ppermute | solution.py:18
  94.8 7.2 %all-to-all-start.1 = ((bf16[16,128,128]{2,1,0:T(8,128)(2,1)}), bf16[16,128,128]{2,1,0:T(8,128)(2,1)}, u32[]{:S(2)}, u32[]{:S(2)}) async-start(bf16[16,128,128]{2,1,0:T(8,128)(2,1)} %bitcast.202), calls=%async_computation.1 | async-start | bytes 1048576 | tf_op jit(solution)/shard_map/all_to_all | solution.py:37
  102.1 1.5 copy.36
  103.6 4.4 %collective-permute-start.12 = (bf16[128,2048]{1,0:T(8,128)(2,1)}, bf16[128,2048]{1,0:T(8,128)(2,1)}, u32[]{:S(2)}, u32[]{:S(2)}) collective-permute-start(bf16[128,2048]{1,0:T(8,128)(2,1)} %collective-permute-done.11), channel_id=1, source_target_pairs={{0,30},{2,0},{4,2},{6,4},{8,6},{10,8},{12,10},{14,12},{16,14},{18,... | collective-permute-start | bytes 1572872 | tf_op jit(solution)/shard_map/ppermute | solution.py:20
  108.0 2.1 multiply_convert_fusion.1
  110.1 3.8 %fusion.58 = f32[16,256,128]{1,2,0:T(8,128)} fusion(bf16[16,256,256]{2,1,0:T(8,128)(2,1)} %multiply_convert_fusion.1, bf16[256,16,128]{0,2,1:T(8,128)(2,1)S(1)} %bitcast.181), kind=kOutput, calls=%fused_computation.186 | convolution fusion | flops 268435456 | bytes 5242880 | tf_op jit(solution)/shard_map/hts,shd->thd/dot_general | solution.py:74
  113.9 3.4 %collective-permute-done.12 = bf16[128,2048]{1,0:T(8,128)(2,1)} collective-permute-done((bf16[128,2048]{1,0:T(8,128)(2,1)}, bf16[128,2048]{1,0:T(8,128)(2,1)}, u32[]{:S(2)}, u32[]{:S(2)}) %collective-permute-start.12) | collective-permute-done | bytes 524320 | tf_op jit(solution)/shard_map/ppermute | solution.py:20
  117.3 4.8 %collective-permute-start.13 = (bf16[128,2048]{1,0:T(8,128)(2,1)}, bf16[128,2048]{1,0:T(8,128)(2,1)}, u32[]{:S(2)}, u32[]{:S(2)}) collective-permute-start(bf16[128,2048]{1,0:T(8,128)(2,1)} %collective-permute-done.12), channel_id=1, source_target_pairs={{0,30},{2,0},{4,2},{6,4},{8,6},{10,8},{12,10},{14,12},{16,14},{18,... | collective-permute-start | bytes 1572872 | tf_op jit(solution)/shard_map/ppermute | solution.py:20
  122.3 2.6 fusion.5
  124.9 5.6 %multiply_convert_fusion = bf16[2048,2048]{1,0:T(8,128)(2,1)} fusion(bf16[256,2048]{0,1:T(8,128)(2,1)S(1)} %bitcast.201, bf16[1,256,2048]{2,1,0:T(8,128)(2,1)S(1)} %copy-done), kind=kOutput, calls=%fused_computation | convolution fusion | flops 2155872256 | bytes 10485760 | tf_op jit(solution)/shard_map/dot_general | solution.py:82
  130.6 4.7 %collective-permute-start.14 = (bf16[128,2048]{1,0:T(8,128)(2,1)}, bf16[128,2048]{1,0:T(8,128)(2,1)S(1)}, u32[]{:S(2)}, u32[]{:S(2)}) collective-permute-start(bf16[128,2048]{1,0:T(8,128)(2,1)} %collective-permute-done.13), channel_id=1, source_target_pairs={{0,30},{2,0},{4,2},{6,4},{8,6},{10,8},{12,10},{14,12},{16,14},{18,... | collective-permute-start | bytes 1572872 | tf_op jit(solution)/shard_map/ppermute | solution.py:20
  136.3 1.2 constant_dynamic-update-slice_fusion.30
  140.9 1.2 constant_dynamic-update-slice_fusion.26
  152.2 1.2 constant_dynamic-update-slice_fusion.15
  165.6 2.5 fusion.2
  169.1 1.3 fusion.8
  170.4 6.6 %all-to-all-start.2 = ((bf16[16,128,128]{2,1,0:T(8,128)(2,1)}), bf16[16,128,128]{2,1,0:T(8,128)(2,1)}, u32[]{:S(2)}, u32[]{:S(2)}) async-start(bf16[16,128,128]{2,1,0:T(8,128)(2,1)} %fusion.8), calls=%async_computation.2 | async-start | bytes 1048576 | tf_op jit(solution)/shard_map/all_to_all | solution.py:29
  177.0 3.4 %multiply_convert_fusion.2 = bf16[16,256,256]{2,1,0:T(8,128)(2,1)} fusion(bf16[256,16,128]{0,2,1:T(8,128)(2,1)} %bitcast.193, bf16[256,16,128]{0,2,1:T(8,128)(2,1)S(1)} %bitcast.182, f32[256,256]{1,0:T(8,128)S(1)} %fusion.21), kind=kOutput, calls=%fused_computation.4 | convolution fusion | flops 270532608 | bytes 4456448 | tf_op jit(solution)/shard_map/the,she->hts/dot_general | solution.py:95
  180.3 3.7 %fusion.57 = f32[16,128,256]{2,1,0:T(8,128)} fusion(bf16[256,16,128]{0,2,1:T(8,128)(2,1)} %bitcast.194, bf16[16,256,256]{2,1,0:T(8,128)(2,1)} %multiply_convert_fusion.1), kind=kOutput, calls=%fused_computation.185 | convolution fusion | flops 268435456 | bytes 5242880 | tf_op jit(solution)/shard_map/hts,the->she/dot_general | solution.py:106
  184.0 16.1 %all-to-all-done.2 = bf16[16,128,128]{2,1,0:T(8,128)(2,1)} async-done(((bf16[16,128,128]{2,1,0:T(8,128)(2,1)}), bf16[16,128,128]{2,1,0:T(8,128)(2,1)}, u32[]{:S(2)}, u32[]{:S(2)}) %all-to-all-start.2) | async-done | bytes 524320 | tf_op jit(solution)/shard_map/all_to_all | solution.py:29
  202.5 11.0 %all-to-all-start.3 = ((bf16[16,128,128]{2,1,0:T(8,128)(2,1)}), bf16[16,128,128]{2,1,0:T(8,128)(2,1)}, u32[]{:S(2)}, u32[]{:S(2)}) async-start(bf16[16,128,128]{2,1,0:T(8,128)(2,1)} %bitcast.203), calls=%async_computation.3 | async-start | bytes 1048576 | tf_op jit(solution)/shard_map/all_to_all | solution.py:37
  213.6 3.8 %fusion.12 = f32[16,256,128]{1,2,0:T(8,128)} fusion(bf16[16,256,256]{2,1,0:T(8,128)(2,1)} %multiply_convert_fusion.2, bf16[256,16,128]{2,1,0:T(8,128)(2,1)S(1)} %bitcast.186), kind=kOutput, calls=%fused_computation.19 | convolution fusion | flops 268435456 | bytes 5242880 | tf_op jit(solution)/shard_map/hts,shd->thd/dot_general | solution.py:98
  217.4 36.6 %reduce-scatter.3.cloned.1.call-done = bf16[128,2048]{1,0:T(8,128)(2,1)} async-done(((bf16[2048,2048]{1,0:T(8,128)(2,1)}), bf16[128,2048]{1,0:T(8,128)(2,1)}) %reduce-scatter.3.cloned.1.call-update) | async-done | bytes 524304 | tf_op jit(solution)/shard_map/reduce_scatter | solution.py:79
  254.0 3.5 %fusion.7 = bf16[256,16,128]{0,2,1:T(8,128)(2,1)} fusion(f32[16,256,128]{1,2,0:T(8,128)} %fusion.12, bf16[16,128,128]{2,1,0:T(8,128)(2,1)} %all-to-all-done.1, bf16[256,16,128]{0,2,1:T(8,128)(2,1)} %bitcast.195), kind=kOutput, calls=%fused_computation.11 | convolution fusion | flops 135266304 | bytes 4718592 | tf_op jit(solution)/shard_map/the,hde->thd/dot_general | solution.py:99
  257.4 2.3 copy.26
  259.7 3.8 %fusion.16 = f32[16,256,128]{1,2,0:T(8,128)} fusion(bf16[16,256,256]{2,1,0:T(8,128)(2,1)} %multiply_convert_fusion.2, bf16[256,16,128]{2,1,0:T(8,128)(2,1)} %bitcast.190), kind=kOutput, calls=%fused_computation.23 | convolution fusion | flops 268435456 | bytes 5242880 | tf_op jit(solution)/shard_map/hts,thd->shd/dot_general | solution.py:102
  263.5 3.2 %add_convert_fusion = bf16[16,128,256]{2,1,0:T(8,128)(2,1)} fusion(f32[16,128,256]{2,1,0:T(8,128)} %fusion.57, bf16[16,128,128]{2,1,0:T(8,128)(2,1)} %all-to-all-done.3, bf16[256,16,128]{2,1,0:T(8,128)(2,1)S(1)} %bitcast.187), kind=kOutput, calls=%fused_computation.12 | convolution fusion | flops 135266304 | bytes 4718592 | tf_op jit(solution)/shard_map/shd,hde->she/dot_general | solution.py:107
  266.8 2.3 copy.28
  269.0 2.2 fusion.6
  271.2 1.4 copy.27
  272.7 1.8 convert_element_type.208
  (107 shorter events, 42.3 us)
Async XLA Ops:
  7.2 117.7 %copy-start = (bf16[1,256,2048]{2,1,0:T(8,128)(2,1)S(1)}, bf16[1,256,2048]{2,1,0:T(8,128)(2,1)}, u32[]{:S(2)}) copy-start(bf16[1,256,2048]{2,1,0:T(8,128)(2,1)} %param.8) | copy-start | bytes 3145732
  11.5 32.9 %all-to-all-start = ((bf16[16,128,128]{2,1,0:T(8,128)(2,1)}), bf16[16,128,128]{2,1,0:T(8,128)(2,1)}, u32[]{:S(2)}, u32[]{:S(2)}) async-start(bf16[16,128,128]{2,1,0:T(8,128)(2,1)} %convolution_convert_fusion.1), calls=%async_computation | async-start | bytes 1048576 | tf_op jit(solution)/shard_map/all_to_all | solution.py:29
  28.4 0.8 copy-start.4
  28.4 11.6 %collective-permute-start = (bf16[128,2048]{1,0:T(8,128)(2,1)S(1)}, bf16[128,2048]{1,0:T(8,128)(2,1)}, u32[]{:S(2)}, u32[]{:S(2)}) collective-permute-start(bf16[128,2048]{1,0:T(8,128)(2,1)S(1)} %all_gather.3), channel_id=1, source_target_pairs={{0,2},{2,4},{4,6},{6,8},{8,10},{10,12},{12,14},{14,16},{16,18},{18... | collective-permute-start | bytes 1572872 | tf_op jit(solution)/shard_map/ppermute | solution.py:18
  29.2 13.4 %collective-permute-start.8 = (bf16[128,2048]{1,0:T(8,128)(2,1)S(1)}, bf16[128,2048]{1,0:T(8,128)(2,1)}, u32[]{:S(2)}, u32[]{:S(2)}) collective-permute-start(bf16[128,2048]{1,0:T(8,128)(2,1)S(1)} %all_gather.3), channel_id=1, source_target_pairs={{0,30},{2,0},{4,2},{6,4},{8,6},{10,8},{12,10},{14,12},{16,14},{18,... | collective-permute-start | bytes 1572872 | tf_op jit(solution)/shard_map/ppermute | solution.py:20
  40.0 11.7 %collective-permute-start.1 = (bf16[128,2048]{1,0:T(8,128)(2,1)}, bf16[128,2048]{1,0:T(8,128)(2,1)}, u32[]{:S(2)}, u32[]{:S(2)}) collective-permute-start(bf16[128,2048]{1,0:T(8,128)(2,1)} %collective-permute-done), channel_id=1, source_target_pairs={{0,2},{2,4},{4,6},{6,8},{8,10},{10,12},{12,14},{14,16},{16,18},{18... | collective-permute-start | bytes 1572872 | tf_op jit(solution)/shard_map/ppermute | solution.py:18
  42.6 24.5 %collective-permute-start.9 = (bf16[128,2048]{1,0:T(8,128)(2,1)}, bf16[128,2048]{1,0:T(8,128)(2,1)}, u32[]{:S(2)}, u32[]{:S(2)}) collective-permute-start(bf16[128,2048]{1,0:T(8,128)(2,1)} %collective-permute-done.8), channel_id=1, source_target_pairs={{0,30},{2,0},{4,2},{6,4},{8,6},{10,8},{12,10},{14,12},{16,14},{18,... | collective-permute-start | bytes 1572872 | tf_op jit(solution)/shard_map/ppermute | solution.py:20
  51.7 11.5 %collective-permute-start.2 = (bf16[128,2048]{1,0:T(8,128)(2,1)}, bf16[128,2048]{1,0:T(8,128)(2,1)S(1)}, u32[]{:S(2)}, u32[]{:S(2)}) collective-permute-start(bf16[128,2048]{1,0:T(8,128)(2,1)} %collective-permute-done.1), channel_id=1, source_target_pairs={{0,2},{2,4},{4,6},{6,8},{8,10},{10,12},{12,14},{14,16},{16,18},{18... | collective-permute-start | bytes 1572872 | tf_op jit(solution)/shard_map/ppermute | solution.py:18
  63.2 31.6 %copy-start.6 = (bf16[128,2048]{1,0:T(8,128)(2,1)}, bf16[128,2048]{1,0:T(8,128)(2,1)S(1)}, u32[]{:S(2)}) copy-start(bf16[128,2048]{1,0:T(8,128)(2,1)S(1)} %collective-permute-done.2) | copy-start | bytes 1572868
  63.2 11.4 %collective-permute-start.3 = (bf16[128,2048]{1,0:T(8,128)(2,1)S(1)}, bf16[128,2048]{1,0:T(8,128)(2,1)S(1)}, u32[]{:S(2)}, u32[]{:S(2)}) collective-permute-start(bf16[128,2048]{1,0:T(8,128)(2,1)S(1)} %collective-permute-done.2), channel_id=1, source_target_pairs={{0,2},{2,4},{4,6},{6,8},{8,10},{10,12},{12,14},{14,16},{16,18},{18... | collective-permute-start | bytes 1572872 | tf_op jit(solution)/shard_map/ppermute | solution.py:18
  67.1 14.1 %collective-permute-start.10 = (bf16[128,2048]{1,0:T(8,128)(2,1)}, bf16[128,2048]{1,0:T(8,128)(2,1)}, u32[]{:S(2)}, u32[]{:S(2)}) collective-permute-start(bf16[128,2048]{1,0:T(8,128)(2,1)} %collective-permute-done.9), channel_id=1, source_target_pairs={{0,30},{2,0},{4,2},{6,4},{8,6},{10,8},{12,10},{14,12},{16,14},{18,... | collective-permute-start | bytes 1572872 | tf_op jit(solution)/shard_map/ppermute | solution.py:20
  74.6 20.2 %copy-start.8 = (bf16[128,2048]{1,0:T(8,128)(2,1)}, bf16[128,2048]{1,0:T(8,128)(2,1)S(1)}, u32[]{:S(2)}) copy-start(bf16[128,2048]{1,0:T(8,128)(2,1)S(1)} %collective-permute-done.3) | copy-start | bytes 1572868
  74.6 11.4 %collective-permute-start.4 = (bf16[128,2048]{1,0:T(8,128)(2,1)S(1)}, bf16[128,2048]{1,0:T(8,128)(2,1)}, u32[]{:S(2)}, u32[]{:S(2)}) collective-permute-start(bf16[128,2048]{1,0:T(8,128)(2,1)S(1)} %collective-permute-done.3), channel_id=1, source_target_pairs={{0,2},{2,4},{4,6},{6,8},{8,10},{10,12},{12,14},{14,16},{16,18},{18... | collective-permute-start | bytes 1572872 | tf_op jit(solution)/shard_map/ppermute | solution.py:18
  81.2 22.4 %collective-permute-start.11 = (bf16[128,2048]{1,0:T(8,128)(2,1)}, bf16[128,2048]{1,0:T(8,128)(2,1)}, u32[]{:S(2)}, u32[]{:S(2)}) collective-permute-start(bf16[128,2048]{1,0:T(8,128)(2,1)} %collective-permute-done.10), channel_id=1, source_target_pairs={{0,30},{2,0},{4,2},{6,4},{8,6},{10,8},{12,10},{14,12},{16,14},{18,... | collective-permute-start | bytes 1572872 | tf_op jit(solution)/shard_map/ppermute | solution.py:20
  86.0 22.0 %collective-permute-start.5 = (bf16[128,2048]{1,0:T(8,128)(2,1)}, bf16[128,2048]{1,0:T(8,128)(2,1)}, u32[]{:S(2)}, u32[]{:S(2)}) collective-permute-start(bf16[128,2048]{1,0:T(8,128)(2,1)} %collective-permute-done.4), channel_id=1, source_target_pairs={{0,2},{2,4},{4,6},{6,8},{8,10},{10,12},{12,14},{14,16},{16,18},{18... | collective-permute-start | bytes 1572872 | tf_op jit(solution)/shard_map/ppermute | solution.py:18
  94.8 27.4 %all-to-all-start.1 = ((bf16[16,128,128]{2,1,0:T(8,128)(2,1)}), bf16[16,128,128]{2,1,0:T(8,128)(2,1)}, u32[]{:S(2)}, u32[]{:S(2)}) async-start(bf16[16,128,128]{2,1,0:T(8,128)(2,1)} %bitcast.202), calls=%async_computation.1 | async-start | bytes 1048576 | tf_op jit(solution)/shard_map/all_to_all | solution.py:37
  102.1 151.9 %reduce-scatter.3.cloned.1.call-start = ((), (), s32[]{:S(2)}) async-start(), calls=%async_computation.6 | async-start | bytes 8912896 | tf_op jit(solution)/shard_map/reduce_scatter | solution.py:79
  103.6 4.4 %copy-start.1 = (bf16[32,8,16,128]{3,2,1,0:T(8,128)(2,1)}, bf16[32,8,16,128]{3,2,1,0:T(8,128)(2,1)S(1)}, u32[]{:S(2)}) copy-start(bf16[32,8,16,128]{3,2,1,0:T(8,128)(2,1)S(1)} %copy.36) | copy-start | bytes 3145732
  103.6 13.6 %collective-permute-start.12 = (bf16[128,2048]{1,0:T(8,128)(2,1)}, bf16[128,2048]{1,0:T(8,128)(2,1)}, u32[]{:S(2)}, u32[]{:S(2)}) collective-permute-start(bf16[128,2048]{1,0:T(8,128)(2,1)} %collective-permute-done.11), channel_id=1, source_target_pairs={{0,30},{2,0},{4,2},{6,4},{8,6},{10,8},{12,10},{14,12},{16,14},{18,... | collective-permute-start | bytes 1572872 | tf_op jit(solution)/shard_map/ppermute | solution.py:20
  108.0 14.3 %collective-permute-start.6 = (bf16[128,2048]{1,0:T(8,128)(2,1)}, bf16[128,2048]{1,0:T(8,128)(2,1)}, u32[]{:S(2)}, u32[]{:S(2)}) collective-permute-start(bf16[128,2048]{1,0:T(8,128)(2,1)} %collective-permute-done.5), channel_id=1, source_target_pairs={{0,2},{2,4},{4,6},{6,8},{8,10},{10,12},{12,14},{14,16},{16,18},{18... | collective-permute-start | bytes 1572872 | tf_op jit(solution)/shard_map/ppermute | solution.py:18
  117.3 13.3 %collective-permute-start.13 = (bf16[128,2048]{1,0:T(8,128)(2,1)}, bf16[128,2048]{1,0:T(8,128)(2,1)}, u32[]{:S(2)}, u32[]{:S(2)}) collective-permute-start(bf16[128,2048]{1,0:T(8,128)(2,1)} %collective-permute-done.12), channel_id=1, source_target_pairs={{0,30},{2,0},{4,2},{6,4},{8,6},{10,8},{12,10},{14,12},{16,14},{18,... | collective-permute-start | bytes 1572872 | tf_op jit(solution)/shard_map/ppermute | solution.py:20
  122.3 13.0 %collective-permute-start.7 = (bf16[128,2048]{1,0:T(8,128)(2,1)}, bf16[128,2048]{1,0:T(8,128)(2,1)}, u32[]{:S(2)}, u32[]{:S(2)}) collective-permute-start(bf16[128,2048]{1,0:T(8,128)(2,1)} %collective-permute-done.6), channel_id=1, source_target_pairs={{0,2},{2,4},{4,6},{6,8},{8,10},{10,12},{12,14},{14,16},{16,18},{18... | collective-permute-start | bytes 1572872 | tf_op jit(solution)/shard_map/ppermute | solution.py:18
  130.5 26.2 %copy-start.9 = (bf16[128,2048]{1,0:T(8,128)(2,1)S(1)}, bf16[128,2048]{1,0:T(8,128)(2,1)}, u32[]{:S(2)}) copy-start(bf16[128,2048]{1,0:T(8,128)(2,1)} %copy-done.8) | copy-start | bytes 1572868
  130.5 26.2 %copy-start.7 = (bf16[128,2048]{1,0:T(8,128)(2,1)S(1)}, bf16[128,2048]{1,0:T(8,128)(2,1)}, u32[]{:S(2)}) copy-start(bf16[128,2048]{1,0:T(8,128)(2,1)} %copy-done.6) | copy-start | bytes 1572868
  130.5 28.4 %copy-start.5 = (bf16[128,2048]{1,0:T(8,128)(2,1)S(1)}, bf16[128,2048]{1,0:T(8,128)(2,1)}, u32[]{:S(2)}) copy-start(bf16[128,2048]{1,0:T(8,128)(2,1)} %copy-done.4) | copy-start | bytes 1572868
  130.6 21.5 %collective-permute-start.14 = (bf16[128,2048]{1,0:T(8,128)(2,1)}, bf16[128,2048]{1,0:T(8,128)(2,1)S(1)}, u32[]{:S(2)}, u32[]{:S(2)}) collective-permute-start(bf16[128,2048]{1,0:T(8,128)(2,1)} %collective-permute-done.13), channel_id=1, source_target_pairs={{0,30},{2,0},{4,2},{6,4},{8,6},{10,8},{12,10},{14,12},{16,14},{18,... | collective-permute-start | bytes 1572872 | tf_op jit(solution)/shard_map/ppermute | solution.py:20
  152.2 17.0 %copy-start.2 = (bf16[32,8,16,128]{3,2,1,0:T(8,128)(2,1)S(1)}, bf16[32,8,16,128]{3,2,1,0:T(8,128)(2,1)}, u32[]{:S(2)}) copy-start(bf16[32,8,16,128]{3,2,1,0:T(8,128)(2,1)} %copy-done.1) | copy-start | bytes 3145732
  168.2 1.0 copy-start.3
  170.4 29.7 %all-to-all-start.2 = ((bf16[16,128,128]{2,1,0:T(8,128)(2,1)}), bf16[16,128,128]{2,1,0:T(8,128)(2,1)}, u32[]{:S(2)}, u32[]{:S(2)}) async-start(bf16[16,128,128]{2,1,0:T(8,128)(2,1)} %fusion.8), calls=%async_computation.2 | async-start | bytes 1048576 | tf_op jit(solution)/shard_map/all_to_all | solution.py:29
  201.7 0.8 copy-start.10
  202.5 61.0 %all-to-all-start.3 = ((bf16[16,128,128]{2,1,0:T(8,128)(2,1)}), bf16[16,128,128]{2,1,0:T(8,128)(2,1)}, u32[]{:S(2)}, u32[]{:S(2)}) async-start(bf16[16,128,128]{2,1,0:T(8,128)(2,1)} %bitcast.203), calls=%async_computation.3 | async-start | bytes 1048576 | tf_op jit(solution)/shard_map/all_to_all | solution.py:37
  213.5 59.1 %reduce-scatter.5.cloned.1.call-start = ((), (), s32[]{:S(2)}) async-start(), calls=%async_computation.7 | async-start | bytes 786432 | tf_op jit(solution)/shard_map/reduce_scatter | solution.py:90
Sparse Core Ops, SparseCore 0:
  130.6 123.2 reduce-scatter.2
  256.2 14.3 reduce-scatter.4
